TPU v7x, 512 devices: a whole 4x8x8 slice. The times are simulated.
512 devices in a mesh: req: 64 (over x, y, core), kv: 8 (over z).
Axes of the slice: x: 4, y: 8, z: 8, core: 2. Of those that a mesh axis runs over, the one named last changes fastest.
Arguments:
- tokens: bfloat16 [64, 4096], P('req'), may hold values from -6 to 6
- attn_gain: float32 [4096], replicated, may hold values from 0.5 to 1.5
- mlp_gain: float32 [4096], replicated, may hold values from 0.5 to 1.5
- w_query: bfloat16 [4096, 4096], P('req', 'kv'), may hold values from -0.09375 to 0.09375
- w_key: bfloat16 [4096, 1024], P('req', 'kv'), may hold values from -0.09375 to 0.09375
- w_value: bfloat16 [4096, 1024], P('req', 'kv'), may hold values from -0.09375 to 0.09375
- w_out: bfloat16 [4096, 4096], P('kv', 'req'), may hold values from -0.09375 to 0.09375
- w_gate: bfloat16 [4096, 14336], P('kv', 'req'), may hold values from -0.09375 to 0.09375
- w_up: bfloat16 [4096, 14336], P('kv', 'req'), may hold values from -0.09375 to 0.09375
- w_down: bfloat16 [14336, 4096], P('req', 'kv'), may hold values from -0.046875 to 0.046875
- cache_keys: bfloat16 [1024, 256, 1024], P('req', None, 'kv')
- cache_values: bfloat16 [1024, 256, 1024], P('req', None, 'kv'), may hold values from -6 to 6
- slot_owner: int32 [1024], P('req'), may hold values from 0 to 63, as said below
- slot_fill: int32 [1024], P('req'), may hold values from 0 to 256, as said below
Outputs:
- out: bfloat16 [64, 4096], P('req', 'kv')
Inputs may be any that keep to these rules, and one draw needn't show every extreme that they name: `slot_owner`: every request owns one slot or more. `slot_fill`: every index of req holds one full slot and one empty slot.
All inputs are finite; a program needn't handle non-finite values.
Results may differ from a plain program's by a relative error of at most 0.013.
The roundings to bfloat16 on the way count: a program that leaves them out, or rounds other values in their place, can miss the bound.
Values may be sent and summed in bfloat16 or wider, within the bound.
A program may use at most 64 MiB of HBM per device.

v0:
```python
import jax
import jax.numpy as jnp
from jax import lax
from jax.sharding import PartitionSpec as P

HQ = 32
HK = 8
DH = 128
EPS = 1e-05
NEG = -1e30


def joined_2(array, axis, combine):
    everything = jax.tree.map(lambda part: lax.all_gather(part, axis), array)
    initial = jax.tree.map(lambda part: part[0], everything)

    def step(k, so_far):
        return combine(so_far, jax.tree.map(lambda part: part[k], everything))

    return lax.fori_loop(1, lax.axis_size(axis), step, initial)


def rms_norm(rows, gain):
    mean = jnp.mean(rows * rows, axis=-1, keepdims=True)
    return (rows * lax.rsqrt(mean + EPS) * gain).astype(jnp.bfloat16)


def combine_parts(first, second):
    highest = jnp.maximum(first[0], second[0])
    left = jnp.exp(first[0] - highest)
    right = jnp.exp(second[0] - highest)
    return (
        highest,
        first[1] * left + second[1] * right,
        first[2] * left[..., None] + second[2] * right[..., None],
    )


def finish_heads(run_max, run_total, run_acc, query, new_key, new_value, scale):
    own_score = (
        jnp.sum(query.astype(jnp.float32) * new_key.astype(jnp.float32)[:, :, None, :], axis=-1)
        * scale
    )
    highest = jnp.maximum(run_max, own_score)
    older = jnp.exp(run_max - highest)
    fresh = jnp.exp(own_score - highest)
    total = run_total * older + fresh
    accum = (
        run_acc * older[..., None] + fresh[..., None] * new_value.astype(jnp.float32)[:, :, None, :]
    )
    return (accum / total[..., None]).astype(jnp.bfloat16).reshape(query.shape[0], -1)


def per_device(
    tokens,
    attn_gain,
    mlp_gain,
    w_query,
    w_key,
    w_value,
    w_out,
    w_gate,
    w_up,
    w_down,
    cache_keys,
    cache_values,
    slot_owner,
    slot_fill,
):
    req_count = lax.axis_size("req")
    kv_count = lax.axis_size("kv")
    local_rows = tokens.shape[0]
    requests = local_rows * req_count
    group = HQ // HK
    kv_local = cache_keys.shape[2] // DH
    scale = DH ** (-0.5)
    resid_in = tokens.astype(jnp.float32)
    normed = rms_norm(resid_in, attn_gain)
    feature_cols = lax.all_to_all(normed, "req", split_axis=1, concat_axis=0, tiled=True)
    joined = jnp.concatenate([w_query, w_key, w_value], axis=1)
    width_q = w_query.shape[1]
    width_k = w_key.shape[1]
    partial_proj = jnp.dot(feature_cols, joined, preferred_element_type=jnp.float32)
    projected = lax.psum(partial_proj, "req").astype(jnp.bfloat16)
    query = projected[:, :width_q].reshape(requests, kv_local, group, DH)
    new_key = projected[:, width_q : width_q + width_k].reshape(requests, kv_local, DH)
    new_value = projected[:, width_q + width_k :].reshape(requests, kv_local, DH)
    slots = cache_keys.shape[0]
    block_len = cache_keys.shape[1]
    keys_four = cache_keys.reshape(slots, block_len, kv_local, DH)
    values_four = cache_values.reshape(slots, block_len, kv_local, DH)
    slot_query = jnp.take(query, slot_owner, axis=0)
    scores = (
        jnp.einsum("skgd,sbkd->skgb", slot_query, keys_four, preferred_element_type=jnp.float32)
        * scale
    )
    valid = (lax.broadcasted_iota(jnp.int32, (slots, block_len), 1) < slot_fill[:, None])[
        :, None, None, :
    ]
    masked = jnp.where(valid, scores, NEG)
    slot_max = jnp.max(masked, axis=-1)
    prob = jnp.where(valid, jnp.exp(masked - slot_max[..., None]), 0.0)
    slot_total = jnp.sum(prob, axis=-1)
    slot_acc = jnp.einsum(
        "skgb,sbkd->skgd",
        prob.astype(jnp.bfloat16),
        values_four,
        preferred_element_type=jnp.float32,
    )
    run_max = jnp.full((requests, kv_local, group), NEG, jnp.float32).at[slot_owner].max(slot_max)
    rescale = jnp.exp(slot_max - run_max[slot_owner])
    run_total = (
        jnp.zeros((requests, kv_local, group), jnp.float32).at[slot_owner].add(slot_total * rescale)
    )
    run_acc = (
        jnp.zeros((requests, kv_local, group, DH), jnp.float32)
        .at[slot_owner]
        .add(slot_acc * rescale[..., None])
    )
    merged_max, merged_total, merged_acc = joined_2(
        (run_max, run_total, run_acc), "req", combine_parts
    )
    heads = finish_heads(merged_max, merged_total, merged_acc, query, new_key, new_value, scale)
    out_part = jnp.dot(heads, w_out, preferred_element_type=jnp.float32)
    head_total = lax.psum(out_part, "kv")
    attn_rows = lax.all_to_all(head_total, "req", split_axis=0, concat_axis=1, tiled=True)
    resid = resid_in + attn_rows
    normed2 = rms_norm(resid, mlp_gain)
    feature_width = normed2.shape[1] // kv_count
    kv_start = lax.axis_index("kv") * feature_width
    feature_block = lax.dynamic_slice_in_dim(normed2, kv_start, feature_width, 1)
    gate_up = jnp.concatenate([w_gate, w_up], axis=1)
    both_parts = jnp.dot(
        lax.all_gather(feature_block, "req", axis=0, tiled=True),
        gate_up,
        preferred_element_type=jnp.float32,
    )
    both_sums = lax.psum_scatter(
        both_parts.astype(jnp.bfloat16), "kv", scatter_dimension=0, tiled=True
    ).astype(jnp.float32)
    hidden_width = w_gate.shape[1]
    hidden = (jax.nn.silu(both_sums[:, :hidden_width]) * both_sums[:, hidden_width:]).astype(
        jnp.bfloat16
    )
    down_parts = jnp.dot(
        lax.all_gather(hidden, "kv", axis=0, tiled=True), w_down, preferred_element_type=jnp.float32
    )
    down_home = lax.psum_scatter(down_parts, "req", scatter_dimension=0, tiled=True)
    resid_block = lax.dynamic_slice_in_dim(resid, kv_start, feature_width, 1)
    return (resid_block + down_home).astype(jnp.bfloat16)


def solution(mesh):
    placed = (
        P("req", None),
        P(),
        P(),
        P("req", "kv"),
        P("req", "kv"),
        P("req", "kv"),
        P("kv", "req"),
        P("kv", "req"),
        P("kv", "req"),
        P("req", "kv"),
        P("req", None, "kv"),
        P("req", None, "kv"),
        P("req"),
        P("req"),
    )
    return jax.shard_map(
        per_device, mesh=mesh, in_specs=placed, out_specs=P("req", "kv"), check_vma=False
    )
```

profile of v0, /device:TPU:1, one launch (start us, length us, event | category | flops | bytes accessed | tf_op | source)
XLA Modules:
  0.0 840.2 jit_solution(18141316335080766035)
XLA Ops:
  6.6 1.5 multiply_reduce_fusion.2
  10.2 11.6 %all-to-all-start = ((bf16[1,64,64]{2,0,1:T(2,128)(2,1)}), bf16[1,64,64]{2,0,1:T(2,128)(2,1)S(1)}, u32[]{:S(2)}, u32[]{:S(2)}) async-start(bf16[1,64,64]{2,0,1:T(2,128)(2,1)} %all_to_all.30), calls=%async_computation | async-start | bytes 65536 | tf_op jit(solution)/shard_map/all_to_all | solution.py:79
  23.9 7.2 all-to-all-done
  32.2 241.8 %all-reduce.5 = bf16[64,768]{1,0:T(8,128)(2,1)S(1)} all-reduce(f32[64,768]{1,0:T(8,128)S(1)} %fusion.10), channel_id=1, replica_groups=mesh['req'=64,'kv'=8] {'req'}, use_global_device_ids=true, to_apply=%region_1.0 | all-reduce | flops 49152 | bytes 294912 | tf_op jit(solution)/shard_map/psum | solution.py:84
  276.4 1.5 convolution_multiply_fusion.1
  281.0 52.1 %all-gather.4 = f32[64,64,4]{1,2,0:T(4,128)S(1)} all-gather(f32[1,64,4]{1,2,0:T(4,128)S(1)} %copy.60), channel_id=3, replica_groups=mesh['req'=64,'kv'=8] {'req'}, dimensions={0}, use_global_device_ids=true | all-gather | bytes 66560 | tf_op jit(solution)/shard_map/all_gather | solution.py:14
  333.1 50.0 %all-gather.3 = f32[64,64,4]{1,2,0:T(4,128)S(1)} all-gather(f32[1,64,4]{1,2,0:T(4,128)S(1)} %copy.59), channel_id=2, replica_groups=mesh['req'=64,'kv'=8] {'req'}, dimensions={0}, use_global_device_ids=true | all-gather | bytes 66560 | tf_op jit(solution)/shard_map/all_gather | solution.py:14
  384.0 100.0 %while.19 = (s32[]{:T(128)}, f32[64,1,4]{0,2,1:T(4,128)S(1)}, f32[64,1,4]{0,2,1:T(4,128)S(1)}, f32[64,1,4,128]{3,2,1,0:T(4,128)S(1)}, f32[64,64,1,4]{1,3,2,0:T(4...) while((s32[]{:T(128)}, f32[64,1,4]{0,2,1:T(4,128)S(1)}, ...), condition=%wide.region_8.9_spmd, body=%wide.region_7.8_spmd.sunk | while | flops 100101 | bytes 412819 | solution.py:20
  384.3 1.3 fusion.60
  385.9 1.3 fusion.60
  387.5 1.3 fusion.60
  389.1 1.3 fusion.60
  390.6 1.3 fusion.60
  392.2 1.3 fusion.60
  393.8 1.3 fusion.60
  484.7 29.5 %psum.15 = f32[64,1,64]{2,0,1:T(8,128)} all-reduce(f32[64,1,64]{2,0,1:T(8,128)S(1)} %convolution_bitcast_fusion), channel_id=1, replica_groups=mesh['req'=64,'kv'=8] {'kv'}, use_global_device_ids=true, to_apply=%region_10.11 | all-reduce | flops 4096 | bytes 32768 | tf_op jit(solution)/shard_map/psum | solution.py:125
  514.3 11.5 %all-to-all-start.1 = ((f32[64,1,64]{2,1,0:T(1,128)}), f32[64,1,64]{2,1,0:T(1,128)S(1)}, u32[]{:S(2)}, u32[]{:S(2)}) async-start(f32[64,1,64]{2,1,0:T(1,128)} %bitcast.23), calls=%async_computation.1 | async-start | bytes 65536 | tf_op jit(solution)/shard_map/all_to_all | solution.py:126
  525.9 9.3 %all-to-all-done.1 = f32[64,1,64]{2,1,0:T(1,128)S(1)} async-done(((f32[64,1,64]{2,1,0:T(1,128)}), f32[64,1,64]{2,1,0:T(1,128)S(1)}, u32[]{:S(2)}, u32[]{:S(2)}) %all-to-all-start.1) | async-done | bytes 16416 | tf_op jit(solution)/shard_map/all_to_all | solution.py:126
  538.5 48.1 %all-gather.5 = bf16[64,1,512]{2,1,0:T(2,128)(2,1)S(1)} all-gather(bf16[1,1,512]{2,1,0:T(2,128)(2,1)S(1)} %fusion.40), channel_id=1, replica_groups=mesh['req'=64,'kv'=8] {'req'}, dimensions={0}, use_global_device_ids=true | all-gather | bytes 66560 | tf_op jit(solution)/shard_map/all_gather | solution.py:134
  587.6 26.7 %reduce-scatter.2.cloned.1.call-done = bf16[8,448]{1,0:T(8,128)(2,1)} async-done(((bf16[64,448]{1,0:T(8,128)(2,1)}), bf16[8,448]{1,0:T(8,128)(2,1)}) %reduce-scatter.2.cloned.1.call-update) | async-done | bytes 7184 | tf_op jit(solution)/shard_map/reduce_scatter | solution.py:138
  615.0 18.3 %all_gather.31 = bf16[64,224]{1,0:T(8,128)(2,1)S(1)} all-gather(bf16[8,224]{1,0:T(8,128)(2,1)S(1)} %fusion.34), channel_id=1, replica_groups=mesh['req'=64,'kv'=8] {'kv'}, dimensions={0}, use_global_device_ids=true | all-gather | bytes 32256 | tf_op jit(solution)/shard_map/all_gather | solution.py:146
  634.2 1.3 dynamic-slice
  635.5 196.2 %all-reduce.4.cloned.1.call-done = f32[64,512]{1,0:T(8,128)} async-done(((f32[64,512]{1,0:T(8,128)}), f32[64,512]{1,0:T(8,128)}) %all-reduce.4.cloned.1.call-update) | async-done | bytes 131088
  831.7 1.9 fusion.41
  (435 shorter events, 105.4 us)
Async XLA Ops:
  6.5 268.1 %copy-start = (bf16[16,256,128]{2,1,0:T(8,128)(2,1)S(1)}, bf16[16,256,128]{2,1,0:T(8,128)(2,1)}, u32[]{:S(2)}) copy-start(bf16[16,256,128]{2,1,0:T(8,128)(2,1)} %param.26) | copy-start | bytes 3145732
  6.5 529.9 %copy-start.3 = (bf16[1,4096]{1,0:T(2,128)(2,1)S(1)}, bf16[1,4096]{1,0:T(2,128)(2,1)}, u32[]{:S(2)}) copy-start(bf16[1,4096]{1,0:T(2,128)(2,1)} %param.16) | copy-start | bytes 24580
  6.5 478.1 %copy-start.4 = (bf16[512,64]{0,1:T(8,128)(2,1)S(1)}, bf16[512,64]{0,1:T(8,128)(2,1)}, u32[]{:S(2)}) copy-start(bf16[512,64]{0,1:T(8,128)(2,1)} %param.22) | copy-start | bytes 196612
  6.5 580.0 %copy-start.5 = (bf16[512,224]{0,1:T(8,128)(2,1)S(1)}, bf16[512,224]{0,1:T(8,128)(2,1)}, u32[]{:S(2)}) copy-start(bf16[512,224]{0,1:T(8,128)(2,1)} %param.24) | copy-start | bytes 688132
  6.5 580.0 %copy-start.6 = (bf16[512,224]{0,1:T(8,128)(2,1)S(1)}, bf16[512,224]{0,1:T(8,128)(2,1)}, u32[]{:S(2)}) copy-start(bf16[512,224]{0,1:T(8,128)(2,1)} %param.23) | copy-start | bytes 688132
  6.5 626.8 %copy-start.2 = (bf16[224,512]{1,0:T(8,128)(2,1)S(1)}, bf16[224,512]{1,0:T(8,128)(2,1)}, u32[]{:S(2)}) copy-start(bf16[224,512]{1,0:T(8,128)(2,1)} %param.25) | copy-start | bytes 688132
  10.2 20.9 %all-to-all-start = ((bf16[1,64,64]{2,0,1:T(2,128)(2,1)}), bf16[1,64,64]{2,0,1:T(2,128)(2,1)S(1)}, u32[]{:S(2)}, u32[]{:S(2)}) async-start(bf16[1,64,64]{2,0,1:T(2,128)(2,1)} %all_to_all.30), calls=%async_computation | async-start | bytes 65536 | tf_op jit(solution)/shard_map/all_to_all | solution.py:79
  21.8 361.3 %all-gather.8.cloned.1.call-start = ((), (), s32[]{:S(2)}) async-start(), calls=%async_computation.4 | async-start | bytes 8519680 | tf_op jit(solution)/shard_map/all_gather | solution.py:14
  279.0 0.7 copy-start.1
  514.3 20.8 %all-to-all-start.1 = ((f32[64,1,64]{2,1,0:T(1,128)}), f32[64,1,64]{2,1,0:T(1,128)S(1)}, u32[]{:S(2)}, u32[]{:S(2)}) async-start(f32[64,1,64]{2,1,0:T(1,128)} %bitcast.23), calls=%async_computation.1 | async-start | bytes 65536 | tf_op jit(solution)/shard_map/all_to_all | solution.py:126
  525.8 88.5 %reduce-scatter.2.cloned.1.call-start = ((), (), s32[]{:S(2)}) async-start(), calls=%async_computation.3 | async-start | bytes 73728 | tf_op jit(solution)/shard_map/reduce_scatter | solution.py:138
  587.5 244.2 %all-reduce.4.cloned.1.call-start = ((), (), s32[]{:S(2)}) async-start(), calls=%async_computation.5 | async-start | bytes 262144
Sparse Core Ops, SparseCore 0:
  279.8 90.5 all-gather.7
  587.6 26.5 reduce-scatter.1
  634.3 197.3 all-reduce.3
where the time goes:
time: 842 us; the launch traced here: 840 us
  blocking collectives  440 us (52%)
  waiting for transfers between devices  239 us (28%)
  other arithmetic  97.7 us (12%)
  starting transfers between devices  23.2 us (3%)
  local copies, waits for them, and re-layouts  18.2 us (2%)
  between operations  14.7 us (2%)
    psum x1, blocking collectives, per_device(): projected = lax.psum(partial_proj, 'req').astype(jnp.bfloat16)  242 us
    unnamed x4, waiting for transfers between devices  196 us
    all_gather x2, blocking collectives, joined_2(): everything = jax.tree.map(lambda part: lax.all_gather(part, axis), array)  102 us
    add x63, other arithmetic, combine_parts(): first[2] * left[..., None] + second[2] * right[..., None]  83.3 us
    all_gather x1, blocking collectives, per_device(): lax.all_gather(feature_block, 'req', axis=0, tiled=True)  48.1 us
    psum x1, blocking collectives, per_device(): head_total = lax.psum(out_part, 'kv')  29.5 us
    reduce_scatter x1, waiting for transfers between devices, per_device(): lax.psum_scatter(both_parts.astype(jnp.bfloat16), 'kv', scatter_dimension...  26.7 us
    all_gather x1, blocking collectives, per_device(): lax.all_gather(hidden, 'kv', axis=0, tiled=True)  18.3 us
  transfers between devices with their start and end apart: 5, of which 4 were waited for; matrix products, arithmetic and copies ran while one was open for 1% of the time, Pallas kernels for 0%

commit v1 on v0

--- a/solution.py
+++ b/solution.py
@@ -131,7 +131,9 @@
     feature_block = lax.dynamic_slice_in_dim(normed2, kv_start, feature_width, 1)
     gate_up = jnp.concatenate([w_gate, w_up], axis=1)
     both_parts = jnp.dot(
-        lax.all_gather(feature_block, "req", axis=0, tiled=True),
+        jnp.concatenate(
+            lax.all_to_all(jnp.stack([feature_block] * lax.axis_size("req")), "req", 0, 0), axis=0
+        ),
         gate_up,
         preferred_element_type=jnp.float32,
     )

time: 842 us -> 808 us (0.960)
  blocking collectives: 440 us -> 405 us
    all_gather x1 -> x0, blocking collectives: 48.1 us -> none  [per_device(): lax.all_gather(feature_block, 'req', axis=0, tiled=True)]
    all_to_all x0 -> x1, blocking collectives: none -> 13.8 us  [per_device(): lax.all_to_all(jnp.stack([feature_block] * lax.axis_size('req')), 'req',...]
where the time goes in v1:
time: 808 us; the launch traced here: 807 us
  blocking collectives  405 us (50%)
  waiting for transfers between devices  238 us (29%)
  other arithmetic  98.7 us (12%)
  starting transfers between devices  23.2 us (3%)
  local copies, waits for them, and re-layouts  18.8 us (2%)
  between operations  14.8 us (2%)
    psum x1, blocking collectives, per_device(): projected = lax.psum(partial_proj, 'req').astype(jnp.bfloat16)  242 us
    unnamed x4, waiting for transfers between devices  196 us
    all_gather x2, blocking collectives, joined_2(): everything = jax.tree.map(lambda part: lax.all_gather(part, axis), array)  102 us
    add x63, other arithmetic, combine_parts(): first[2] * left[..., None] + second[2] * right[..., None]  83.3 us
    psum x1, blocking collectives, per_device(): head_total = lax.psum(out_part, 'kv')  29.5 us
    reduce_scatter x1, waiting for transfers between devices, per_device(): lax.psum_scatter(both_parts.astype(jnp.bfloat16), 'kv', scatter_dimension...  25.5 us
    all_gather x1, blocking collectives, per_device(): lax.all_gather(hidden, 'kv', axis=0, tiled=True)  18.3 us
  transfers between devices with their start and end apart: 5, of which 4 were waited for; matrix products, arithmetic and copies ran while one was open for 1% of the time, Pallas kernels for 0%

profile of v1, /device:TPU:1, one launch (start us, length us, event | category | flops | bytes accessed | tf_op | source)
XLA Modules:
  0.0 806.6 jit_solution(7552972818271201791)
XLA Ops:
  6.6 1.5 multiply_reduce_fusion.2
  10.2 11.6 %all-to-all-start = ((bf16[1,64,64]{2,0,1:T(2,128)(2,1)}), bf16[1,64,64]{2,0,1:T(2,128)(2,1)S(1)}, u32[]{:S(2)}, u32[]{:S(2)}) async-start(bf16[1,64,64]{2,0,1:T(2,128)(2,1)} %all_to_all.34), calls=%async_computation | async-start | bytes 65536 | tf_op jit(solution)/shard_map/all_to_all | solution.py:79
  23.9 7.2 all-to-all-done
  32.2 241.8 %all-reduce.5 = bf16[64,768]{1,0:T(8,128)(2,1)S(1)} all-reduce(f32[64,768]{1,0:T(8,128)S(1)} %fusion.10), channel_id=1, replica_groups=mesh['req'=64,'kv'=8] {'req'}, use_global_device_ids=true, to_apply=%region_1.0 | all-reduce | flops 49152 | bytes 294912 | tf_op jit(solution)/shard_map/psum | solution.py:84
  276.4 1.5 convolution_multiply_fusion.1
  281.0 52.1 %all-gather.4 = f32[64,64,4]{1,2,0:T(4,128)S(1)} all-gather(f32[1,64,4]{1,2,0:T(4,128)S(1)} %copy.60), channel_id=3, replica_groups=mesh['req'=64,'kv'=8] {'req'}, dimensions={0}, use_global_device_ids=true | all-gather | bytes 66560 | tf_op jit(solution)/shard_map/all_gather | solution.py:14
  333.1 50.0 %all-gather.3 = f32[64,64,4]{1,2,0:T(4,128)S(1)} all-gather(f32[1,64,4]{1,2,0:T(4,128)S(1)} %copy.59), channel_id=2, replica_groups=mesh['req'=64,'kv'=8] {'req'}, dimensions={0}, use_global_device_ids=true | all-gather | bytes 66560 | tf_op jit(solution)/shard_map/all_gather | solution.py:14
  384.0 100.0 %while.19 = (s32[]{:T(128)}, f32[64,1,4]{0,2,1:T(4,128)S(1)}, f32[64,1,4]{0,2,1:T(4,128)S(1)}, f32[64,1,4,128]{3,2,1,0:T(4,128)S(1)}, f32[64,64,1,4]{1,3,2,0:T(4...) while((s32[]{:T(128)}, f32[64,1,4]{0,2,1:T(4,128)S(1)}, ...), condition=%wide.region_8.9_spmd, body=%wide.region_7.8_spmd.sunk | while | flops 100101 | bytes 412819 | solution.py:20
  384.3 1.3 fusion.60
  385.9 1.3 fusion.60
  387.5 1.3 fusion.60
  389.1 1.3 fusion.60
  390.6 1.3 fusion.60
  392.2 1.3 fusion.60
  393.8 1.3 fusion.60
  484.7 29.5 %psum.15 = f32[64,1,64]{2,0,1:T(8,128)} all-reduce(f32[64,1,64]{2,0,1:T(8,128)S(1)} %convolution_bitcast_fusion), channel_id=1, replica_groups=mesh['req'=64,'kv'=8] {'kv'}, use_global_device_ids=true, to_apply=%region_10.11 | all-reduce | flops 4096 | bytes 32768 | tf_op jit(solution)/shard_map/psum | solution.py:125
  514.3 11.5 %all-to-all-start.1 = ((f32[64,1,64]{2,1,0:T(1,128)}), f32[64,1,64]{2,1,0:T(1,128)S(1)}, u32[]{:S(2)}, u32[]{:S(2)}) async-start(f32[64,1,64]{2,1,0:T(1,128)} %bitcast.23), calls=%async_computation.1 | async-start | bytes 65536 | tf_op jit(solution)/shard_map/all_to_all | solution.py:126
  525.9 9.3 %all-to-all-done.1 = f32[64,1,64]{2,1,0:T(1,128)S(1)} async-done(((f32[64,1,64]{2,1,0:T(1,128)}), f32[64,1,64]{2,1,0:T(1,128)S(1)}, u32[]{:S(2)}, u32[]{:S(2)}) %all-to-all-start.1) | async-done | bytes 16416 | tf_op jit(solution)/shard_map/all_to_all | solution.py:126
  540.1 13.8 %all_to_all.38 = bf16[64,2,256]{2,1,0:T(2,128)(2,1)S(1)} all-to-all(bf16[64,2,256]{2,1,0:T(2,128)(2,1)S(1)} %reshape.317), channel_id=1, replica_groups=mesh['req'=64,'kv'=8] {'req'}, dimensions={0} | all-to-all | bytes 131072 | tf_op jit(solution)/shard_map/all_to_all | solution.py:135
  554.9 25.5 %reduce-scatter.2.cloned.1.call-done = bf16[8,448]{1,0:T(8,128)(2,1)} async-done(((bf16[64,448]{1,0:T(8,128)(2,1)}), bf16[8,448]{1,0:T(8,128)(2,1)}) %reduce-scatter.2.cloned.1.call-update) | async-done | bytes 7184 | tf_op jit(solution)/shard_map/reduce_scatter | solution.py:140
  581.2 18.3 %all_gather.27 = bf16[64,224]{1,0:T(8,128)(2,1)S(1)} all-gather(bf16[8,224]{1,0:T(8,128)(2,1)S(1)} %fusion.34), channel_id=1, replica_groups=mesh['req'=64,'kv'=8] {'kv'}, dimensions={0}, use_global_device_ids=true | all-gather | bytes 32256 | tf_op jit(solution)/shard_map/all_gather | solution.py:148
  600.4 1.3 dynamic-slice
  601.7 196.4 %all-reduce.4.cloned.1.call-done = f32[64,512]{1,0:T(8,128)} async-done(((f32[64,512]{1,0:T(8,128)}), f32[64,512]{1,0:T(8,128)}) %all-reduce.4.cloned.1.call-update) | async-done | bytes 131088
  798.1 1.9 fusion.40
  (440 shorter events, 107.1 us)
Async XLA Ops:
  6.5 268.1 %copy-start = (bf16[16,256,128]{2,1,0:T(8,128)(2,1)S(1)}, bf16[16,256,128]{2,1,0:T(8,128)(2,1)}, u32[]{:S(2)}) copy-start(bf16[16,256,128]{2,1,0:T(8,128)(2,1)} %param.26) | copy-start | bytes 3145732
  6.5 529.9 %copy-start.3 = (bf16[1,4096]{1,0:T(2,128)(2,1)S(1)}, bf16[1,4096]{1,0:T(2,128)(2,1)}, u32[]{:S(2)}) copy-start(bf16[1,4096]{1,0:T(2,128)(2,1)} %param.16) | copy-start | bytes 24580
  6.5 478.1 %copy-start.4 = (bf16[512,64]{0,1:T(8,128)(2,1)S(1)}, bf16[512,64]{0,1:T(8,128)(2,1)}, u32[]{:S(2)}) copy-start(bf16[512,64]{0,1:T(8,128)(2,1)} %param.22) | copy-start | bytes 196612
  6.5 547.4 %copy-start.5 = (bf16[512,224]{0,1:T(8,128)(2,1)S(1)}, bf16[512,224]{0,1:T(8,128)(2,1)}, u32[]{:S(2)}) copy-start(bf16[512,224]{0,1:T(8,128)(2,1)} %param.24) | copy-start | bytes 688132
  6.5 547.4 %copy-start.6 = (bf16[512,224]{0,1:T(8,128)(2,1)S(1)}, bf16[512,224]{0,1:T(8,128)(2,1)}, u32[]{:S(2)}) copy-start(bf16[512,224]{0,1:T(8,128)(2,1)} %param.23) | copy-start | bytes 688132
  6.5 593.0 %copy-start.2 = (bf16[224,512]{1,0:T(8,128)(2,1)S(1)}, bf16[224,512]{1,0:T(8,128)(2,1)}, u32[]{:S(2)}) copy-start(bf16[224,512]{1,0:T(8,128)(2,1)} %param.25) | copy-start | bytes 688132
  10.2 20.9 %all-to-all-start = ((bf16[1,64,64]{2,0,1:T(2,128)(2,1)}), bf16[1,64,64]{2,0,1:T(2,128)(2,1)S(1)}, u32[]{:S(2)}, u32[]{:S(2)}) async-start(bf16[1,64,64]{2,0,1:T(2,128)(2,1)} %all_to_all.34), calls=%async_computation | async-start | bytes 65536 | tf_op jit(solution)/shard_map/all_to_all | solution.py:79
  21.8 361.3 %all-gather.7.cloned.1.call-start = ((), (), s32[]{:S(2)}) async-start(), calls=%async_computation.5 | async-start | bytes 8519680 | tf_op jit(solution)/shard_map/all_gather | solution.py:14
  279.0 0.7 copy-start.1
  514.3 20.8 %all-to-all-start.1 = ((f32[64,1,64]{2,1,0:T(1,128)}), f32[64,1,64]{2,1,0:T(1,128)S(1)}, u32[]{:S(2)}, u32[]{:S(2)}) async-start(f32[64,1,64]{2,1,0:T(1,128)} %bitcast.23), calls=%async_computation.1 | async-start | bytes 65536 | tf_op jit(solution)/shard_map/all_to_all | solution.py:126
  525.8 54.7 %reduce-scatter.2.cloned.1.call-start = ((), (), s32[]{:S(2)}) async-start(), calls=%async_computation.4 | async-start | bytes 73728 | tf_op jit(solution)/shard_map/reduce_scatter | solution.py:140
  554.9 243.2 %all-reduce.4.cloned.1.call-start = ((), (), s32[]{:S(2)}) async-start(), calls=%async_computation.6 | async-start | bytes 262144
Sparse Core Ops, SparseCore 0:
  279.8 90.5 all-gather.6
  555.0 25.4 reduce-scatter.1
  600.5 197.5 all-reduce.3
